TPU v7x, 32 devices: a whole 2x2x4 slice. The times are simulated.
32 devices in a mesh: groups: 2 (over x), asset: 16 (over z, y, core).
Axes of the slice: x: 2, y: 2, z: 4, core: 2. Of those that a mesh axis runs over, the one named last changes fastest.
Arguments:
- scen_draws: bfloat16 [8192, 256], P(('groups', 'asset')), parts along dimension 0, may hold values from -4 to 4
- factor_mix: bfloat16 [256, 256], replicated, may hold values from -0.375 to 0.375
- loadings: bfloat16 [32768, 256], P(('groups', 'asset')), parts along dimension 0, may hold values from -0.375 to 0.375
- convexity: float32 [32768], P(('groups', 'asset')), parts along dimension 0, may hold values from -0.6 to 0.6
- holdings: float32 [32768], P(('groups', 'asset')), parts along dimension 0, may hold values from -0.22097087 to 0.22097087
- desk_map: int32 [32768], P(('groups', 'asset')), parts along dimension 0, may hold values from 0 to 127
- ranks: int32 [8192], P('groups'), parts along dimension 0, may hold values from 0 to 4095, each once
- desk_prices: float32 [256], P('groups'), parts along dimension 0, may hold values from -5 to 5
Outputs:
- allocation: float32 [256], P('groups'), parts along dimension 0
- grad_loadings: float32 [32768, 256], P(('groups', 'asset')), parts along dimension 0
- grad_convexity: float32 [32768], P(('groups', 'asset')), parts along dimension 0
There are 2 independent parts, one for each index of `groups`. A program takes and returns all parts, laid end to end along the dimension named above; an argument that names none is the same for every part. Nothing has to cross between parts.
All inputs are finite; a program needn't handle non-finite values.
Results may differ from a plain program's by a relative error of at most 0.0029.
Values may be sent and summed in bfloat16 or wider, within the bound.
A program may use at most 64 MiB of HBM per device.

v0:
```python
import math
import jax
import jax.numpy as jnp
from jax import lax
from jax.sharding import PartitionSpec as P

DESKS = 128
BAND = 32
CENTER = 166


def smooth_bend(value):
    return jnp.logaddexp(value, -value) - math.log(2.0)


def rank_kernel(ranks, scenarios):
    centre = jnp.float32(CENTER)
    spread = jnp.float32(BAND)
    offsets = (ranks.astype(jnp.float32) - centre) / spread
    every = (jnp.arange(scenarios, dtype=jnp.float32) - centre) / spread
    return jnp.exp(-0.5 * offsets * offsets) / jnp.sum(jnp.exp(-0.5 * every * every))


def cotangent_of(
    weights,
    weight_total,
    slopes,
    smoothing,
    kernel,
    grad_quant,
    grad_band,
    centred,
    prices,
    scenarios,
):
    grad_loss = (
        slopes / smoothing
        + kernel * grad_quant
        + grad_band * 0.09 * centred / (scenarios * smoothing)
    )
    return (
        scenarios * (-weights[:, None] * prices[None, :] / weight_total - grad_loss[:, None])
    ).astype(jnp.bfloat16)


def tail_core(losses, valued, ranks, prices):
    scenarios = losses.shape[0]
    kernel = rank_kernel(ranks, scenarios)
    quantile = jnp.sum(kernel * losses)
    average = jnp.mean(losses)
    centred = losses - average
    smoothing = 0.3 * jnp.sqrt(jnp.mean(centred * centred) + 1e-06)
    scores = (losses - quantile) / smoothing
    weights = jax.nn.sigmoid(scores)
    weight_total = jnp.sum(weights)
    objective = -jnp.sum(weights * valued) / weight_total
    slopes = (-valued - objective) / weight_total * weights * (1.0 - weights)
    grad_quant = -jnp.sum(slopes) / smoothing
    grad_band = -jnp.sum(slopes * scores) / smoothing
    cotangent = cotangent_of(
        weights,
        weight_total,
        slopes,
        smoothing,
        kernel,
        grad_quant,
        grad_band,
        centred,
        prices,
        scenarios,
    )
    return (cotangent, weights, weight_total)


def tail_terms(desk_pnl, ranks, prices):
    losses = -jnp.sum(desk_pnl, axis=1)
    valued = jnp.sum(desk_pnl * prices[None, :], axis=1)
    cotangent, weights, weight_total = tail_core(losses, valued, ranks, prices)
    allocation = -jnp.sum(weights[:, None] * desk_pnl, axis=0) / weight_total
    return (cotangent, allocation)


def desk_table(desk_map):
    columns = jnp.arange(DESKS, dtype=jnp.int32)
    return (desk_map[:, None] == columns[None, :]).astype(jnp.bfloat16)


def split_rows(array, block_rows):
    return array.reshape((-1, block_rows) + array.shape[1:])


def exposure_of(shock_rows, loadings):
    return lax.dot_general(
        shock_rows, loadings, (((1,), (1,)), ((), ())), preferred_element_type=jnp.float32
    )


def pnl_rows(shock_rows, loadings, convexity, holdings, table):
    number = shock_rows.shape[0]
    block_rows = math.gcd(number, 512)

    def pnl_one_block(shock_block):
        exposure = exposure_of(shock_block, loadings)
        held = (holdings * (exposure + convexity * smooth_bend(exposure))).astype(jnp.bfloat16)
        return jnp.dot(held, table, preferred_element_type=jnp.float32)

    result = lax.map(pnl_one_block, split_rows(shock_rows, block_rows))
    return result.reshape((number, table.shape[1]))


def grad_rows(carry, shock_rows, cot_rows, loadings, convexity, holdings, table):
    number = shock_rows.shape[0]
    block_rows = math.gcd(number, 512)

    def grad_one_block(state, inputs):
        shock_block, cot_block = inputs
        exposure = exposure_of(shock_block, loadings)
        spread_back = lax.dot_general(
            cot_block, table, (((1,), (1,)), ((), ())), preferred_element_type=jnp.float32
        )
        held = holdings * spread_back
        grad_exposure = (held * (1.0 + convexity * jnp.tanh(exposure))).astype(jnp.bfloat16)
        grad_load = state[0] + lax.dot_general(
            grad_exposure, shock_block, (((0,), (0,)), ((), ())), preferred_element_type=jnp.float32
        )
        grad_conv = state[1] + jnp.sum(held * smooth_bend(exposure), axis=0)
        return ((grad_load, grad_conv), None)

    final, ignored = lax.scan(
        grad_one_block,
        carry,
        (split_rows(shock_rows, block_rows), split_rows(cot_rows, block_rows)),
    )
    return final


def shards(scen_draws, factor_mix, loadings, convexity, holdings, desk_map, ranks, desk_prices):
    local_shocks = jnp.dot(scen_draws, factor_mix, preferred_element_type=jnp.float32).astype(
        jnp.bfloat16
    )
    table = desk_table(desk_map)
    shocks = lax.all_gather(local_shocks, "asset", axis=0, tiled=True)
    partial_value = pnl_rows(shocks, loadings, convexity, holdings, table)
    desk_pnl = lax.psum(partial_value, "asset")
    cotangent, allocation = tail_terms(desk_pnl, ranks, desk_prices)
    initial = (
        jnp.zeros((loadings.shape[0], loadings.shape[1]), jnp.float32),
        jnp.zeros((loadings.shape[0],), jnp.float32),
    )
    grad_load, grad_conv = grad_rows(
        initial, shocks, cotangent, loadings, convexity, holdings, table
    )
    squares = lax.psum(jnp.sum(grad_load * grad_load) + jnp.sum(grad_conv * grad_conv), "asset")
    entries = loadings.shape[0] * lax.axis_size("asset") * (loadings.shape[1] + 1)
    factor = lax.rsqrt(squares / entries + 1e-06)
    return (allocation, grad_load * factor, grad_conv * factor)


def solution(mesh):
    placed = (
        P(("groups", "asset"), None),
        P(),
        P(("groups", "asset"), None),
        P(("groups", "asset")),
        P(("groups", "asset")),
        P(("groups", "asset")),
        P("groups"),
        P("groups"),
    )
    return jax.shard_map(
        shards,
        mesh=mesh,
        in_specs=placed,
        out_specs=(P("groups"), P(("groups", "asset"), None), P(("groups", "asset"))),
        check_vma=False,
    )
```

profile of v0, /device:TPU:0, one launch (start us, length us, event | category | flops | bytes accessed | tf_op | source)
XLA Modules:
  0.0 288.6 jit_solution(887370904575663468)
XLA Ops:
  7.2 0.0 all-gather.2.cloned.1.call-start
  7.2 0.8 copy-done
  8.1 1.7 convolution_convert_fusion
  9.8 0.0 all-reduce.2.cloned.1.call-start
  9.9 45.0 %all-gather.2.cloned.1.call-done = bf16[4096,256]{1,0:T(8,128)(2,1)} async-done(((bf16[256,256]{1,0:T(8,128)(2,1)}), bf16[4096,256]{1,0:T(8,128)(2,1)}) %all-gather.2.cloned.1.call-update) | async-done | bytes 2097168 | tf_op jit(solution)/shard_map/all_gather | solution.py:142
  54.9 30.3 %while.28 = (s32[]{:T(128)}, f32[8,512,128]{2,1,0:T(8,128)}, f32[1024]{0:T(1024)}, bf16[8,512,256]{2,1,0:T(8,128)(2,1)}, bf16[1024,256]{1,0:T(8,128)(2,1)}, /*index=5*/f32[1024]{0:T(1024)}, s32[1024]{0:T(1024)}, s32[]{:T(128)}) while((s32[]{:T(128)}, f32[8,512,128]{2,1,0:T(8,128)}, f32[1024]{0:T(1024)}, ...), condition=%wide.region_1.2_spmd.clone, body=%wide.region_0.1_spmd.clone.sunk | while | flops 410255360 | bytes 1061981 | solution.py:107
  54.9 3.8 %fusion.70 = f32[8,512,128]{2,1,0:T(8,128)} fusion(f32[8,512,128]{2,1,0:T(8,128)} %get-tuple-element.417, s32[]{:T(128)S(6)} %copy.14, bf16[1024,256]{1,0:T(8,128)(2,1)} %get-tuple-element.428, f32[1024]{0:T(1024)} %get-tuple-element.429, f32[1024]{0:T(1024)} %get-tuple-element.426, s32[1024]{0:T(1024)} %get-tuple-element.430, ...), kind=kOutput, calls=%fused_computation.14.clone.1 | convolution fusion | flops 410255360 | bytes 1061888 | tf_op jit(solution)/shard_map/while/body/eval_jaxpr/dot_general | solution.py:105
  58.7 3.8 %fusion.70 = f32[8,512,128]{2,1,0:T(8,128)} fusion(f32[8,512,128]{2,1,0:T(8,128)} %get-tuple-element.417, s32[]{:T(128)S(6)} %copy.14, bf16[1024,256]{1,0:T(8,128)(2,1)} %get-tuple-element.428, f32[1024]{0:T(1024)} %get-tuple-element.429, f32[1024]{0:T(1024)} %get-tuple-element.426, s32[1024]{0:T(1024)} %get-tuple-element.430, ...), kind=kOutput, calls=%fused_computation.14.clone.1 | convolution fusion | flops 410255360 | bytes 1061888 | tf_op jit(solution)/shard_map/while/body/eval_jaxpr/dot_general | solution.py:105
  62.5 3.8 %fusion.70 = f32[8,512,128]{2,1,0:T(8,128)} fusion(f32[8,512,128]{2,1,0:T(8,128)} %get-tuple-element.417, s32[]{:T(128)S(6)} %copy.14, bf16[1024,256]{1,0:T(8,128)(2,1)} %get-tuple-element.428, f32[1024]{0:T(1024)} %get-tuple-element.429, f32[1024]{0:T(1024)} %get-tuple-element.426, s32[1024]{0:T(1024)} %get-tuple-element.430, ...), kind=kOutput, calls=%fused_computation.14.clone.1 | convolution fusion | flops 410255360 | bytes 1061888 | tf_op jit(solution)/shard_map/while/body/eval_jaxpr/dot_general | solution.py:105
  66.3 3.8 %fusion.70 = f32[8,512,128]{2,1,0:T(8,128)} fusion(f32[8,512,128]{2,1,0:T(8,128)} %get-tuple-element.417, s32[]{:T(128)S(6)} %copy.14, bf16[1024,256]{1,0:T(8,128)(2,1)} %get-tuple-element.428, f32[1024]{0:T(1024)} %get-tuple-element.429, f32[1024]{0:T(1024)} %get-tuple-element.426, s32[1024]{0:T(1024)} %get-tuple-element.430, ...), kind=kOutput, calls=%fused_computation.14.clone.1 | convolution fusion | flops 410255360 | bytes 1061888 | tf_op jit(solution)/shard_map/while/body/eval_jaxpr/dot_general | solution.py:105
  70.1 3.8 %fusion.70 = f32[8,512,128]{2,1,0:T(8,128)} fusion(f32[8,512,128]{2,1,0:T(8,128)} %get-tuple-element.417, s32[]{:T(128)S(6)} %copy.14, bf16[1024,256]{1,0:T(8,128)(2,1)} %get-tuple-element.428, f32[1024]{0:T(1024)} %get-tuple-element.429, f32[1024]{0:T(1024)} %get-tuple-element.426, s32[1024]{0:T(1024)} %get-tuple-element.430, ...), kind=kOutput, calls=%fused_computation.14.clone.1 | convolution fusion | flops 410255360 | bytes 1061888 | tf_op jit(solution)/shard_map/while/body/eval_jaxpr/dot_general | solution.py:105
  73.8 3.8 %fusion.70 = f32[8,512,128]{2,1,0:T(8,128)} fusion(f32[8,512,128]{2,1,0:T(8,128)} %get-tuple-element.417, s32[]{:T(128)S(6)} %copy.14, bf16[1024,256]{1,0:T(8,128)(2,1)} %get-tuple-element.428, f32[1024]{0:T(1024)} %get-tuple-element.429, f32[1024]{0:T(1024)} %get-tuple-element.426, s32[1024]{0:T(1024)} %get-tuple-element.430, ...), kind=kOutput, calls=%fused_computation.14.clone.1 | convolution fusion | flops 410255360 | bytes 1061888 | tf_op jit(solution)/shard_map/while/body/eval_jaxpr/dot_general | solution.py:105
  77.6 3.8 %fusion.70 = f32[8,512,128]{2,1,0:T(8,128)} fusion(f32[8,512,128]{2,1,0:T(8,128)} %get-tuple-element.417, s32[]{:T(128)S(6)} %copy.14, bf16[1024,256]{1,0:T(8,128)(2,1)} %get-tuple-element.428, f32[1024]{0:T(1024)} %get-tuple-element.429, f32[1024]{0:T(1024)} %get-tuple-element.426, s32[1024]{0:T(1024)} %get-tuple-element.430, ...), kind=kOutput, calls=%fused_computation.14.clone.1 | convolution fusion | flops 410255360 | bytes 1061888 | tf_op jit(solution)/shard_map/while/body/eval_jaxpr/dot_general | solution.py:105
  81.4 3.8 %fusion.70 = f32[8,512,128]{2,1,0:T(8,128)} fusion(f32[8,512,128]{2,1,0:T(8,128)} %get-tuple-element.417, s32[]{:T(128)S(6)} %copy.14, bf16[1024,256]{1,0:T(8,128)(2,1)} %get-tuple-element.428, f32[1024]{0:T(1024)} %get-tuple-element.429, f32[1024]{0:T(1024)} %get-tuple-element.426, s32[1024]{0:T(1024)} %get-tuple-element.430, ...), kind=kOutput, calls=%fused_computation.14.clone.1 | convolution fusion | flops 410255360 | bytes 1061888 | tf_op jit(solution)/shard_map/while/body/eval_jaxpr/dot_general | solution.py:105
  85.2 0.0 all-reduce.2.cloned.1.call-update
  85.2 0.6 exponential_reduce_fusion
  85.9 96.4 %all-reduce.2.cloned.1.call-done = f32[4096,128]{1,0:T(8,128)} async-done(((f32[4096,128]{1,0:T(8,128)}), f32[4096,128]{1,0:T(8,128)}) %all-reduce.2.cloned.1.call-update) | async-done | bytes 2097168 | tf_op jit(solution)/shard_map/psum | solution.py:144
  182.2 3.0 %fusion.50 = (f32[]{:T(128)}, f32[4096]{0:T(1024)S(1)}) fusion(f32[4096,128]{1,0:T(8,128)} %all-reduce.2.cloned.1.call-done), kind=kLoop, calls=%fused_computation.73 | loop fusion | flops 1044479 | bytes 2113540 | tf_op jit(solution)/shard_map/reduce_sum | solution.py:50
  185.9 1.3 multiply_reduce_fusion.6
  187.9 0.7 fusion.52
  188.6 1.3 multiply_reduce_fusion
  189.9 0.6 multiply_reduce_fusion.4
  191.8 1.9 fusion.51
  195.0 0.7 divide_add_fusion
  195.7 1.9 multiply_convert_fusion.2
  197.6 47.0 %while.29 = (s32[]{:T(128)}, f32[1024,256]{1,0:T(8,128)S(1)}, f32[1024]{0:T(1024)S(1)}, f32[1024]{0:T(1024)S(1)}, bf16[8,512,128]{2,1,0:T(8,128)(2,1)S(1)}, /*in...) while((s32[]{:T(128)}, f32[1024,256]{1,0:T(8,128)S(1)}, ...), condition=%wide.region_16.17_spmd.clone, body=%wide.region_14.16_spmd.clone.sunk | while | flops 681313280 | bytes 15892648 | solution.py:129
  197.6 0.6 fusion.75
  198.2 0.5 copy-done.7
  198.7 2.8 fusion.76
  201.4 2.0 convolution_add_fusion.2
  203.5 0.6 fusion.75
  204.1 0.5 copy-done.7
  204.5 2.8 fusion.76
  207.3 2.0 convolution_add_fusion.2
  209.4 0.6 fusion.75
  209.9 0.5 copy-done.7
  210.4 2.8 fusion.76
  213.2 2.0 convolution_add_fusion.2
  215.3 0.6 fusion.75
  215.8 0.5 copy-done.7
  216.3 2.8 fusion.76
  219.1 2.0 convolution_add_fusion.2
  221.1 0.6 fusion.75
  221.7 0.5 copy-done.7
  222.2 2.8 fusion.76
  225.0 2.0 convolution_add_fusion.2
  227.0 0.6 fusion.75
  227.6 0.5 copy-done.7
  228.1 2.8 fusion.76
  230.8 2.0 convolution_add_fusion.2
  232.9 0.6 fusion.75
  233.5 0.5 copy-done.7
  233.9 2.8 fusion.76
  236.7 2.0 convolution_add_fusion.2
  238.8 0.6 fusion.75
  239.4 0.5 copy-done.7
  239.8 2.8 fusion.76
  242.6 2.0 convolution_add_fusion.2
  244.7 0.9 multiply_reduce_fusion.2
  245.5 0.6 multiply_reduce_fusion.7
  247.4 30.9 %psum.15 = f32[]{:T(128)} all-reduce(f32[]{:T(128)S(6)} %add.106), channel_id=1, replica_groups=mesh['groups'=2,'asset'=16] {'asset'}, use_global_device_ids=true, to_apply=%region_19.20 | all-reduce | flops 1 | bytes 8 | tf_op jit(solution)/shard_map/psum | solution.py:153
  279.0 0.6 broadcast_multiply_fusion.1
  279.6 1.0 broadcast_multiply_fusion
  280.7 1.1 negate_divide_fusion
  (35 shorter events, 0.1 us)
Async XLA Ops:
  7.2 0.9 copy-start
  7.2 47.8 %all-gather.2.cloned.1.call-start = ((), (), s32[]{:S(2)}) async-start(), calls=%async_computation | async-start | bytes 2228224 | tf_op jit(solution)/shard_map/all_gather | solution.py:142
  9.8 172.4 %all-reduce.2.cloned.1.call-start = ((), (), s32[]{:S(2)}) async-start(), calls=%async_computation.1 | async-start | bytes 4194304 | tf_op jit(solution)/shard_map/psum | solution.py:144
  85.2 100.7 %copy-start.5 = (s32[4096]{0:T(1024)S(1)}, s32[4096]{0:T(1024)}, u32[]{:S(2)}) copy-start(s32[4096]{0:T(1024)} %param.18) | copy-start | bytes 49156
  85.2 103.4 %copy-start.6 = (f32[128]{0:T(128)S(1)}, f32[128]{0:T(128)}, u32[]{:S(2)}) copy-start(f32[128]{0:T(128)} %param.19) | copy-start | bytes 1540
  182.2 6.3 %copy-start.1 = (f32[4096,128]{1,0:T(8,128)S(1)}, f32[4096,128]{1,0:T(8,128)}, u32[]{:S(2)}) copy-start(f32[4096,128]{1,0:T(8,128)} %all-reduce.2.cloned.1.call-done) | copy-start | bytes 6291460
  185.2 12.4 %copy-start.2 = (s32[1024]{0:T(1024)S(1)}, s32[1024]{0:T(1024)}, u32[]{:S(2)}) copy-start(s32[1024]{0:T(1024)} %get-tuple-element.474) | copy-start | bytes 12292
  185.2 12.4 %copy-start.3 = (f32[1024]{0:T(1024)S(1)}, f32[1024]{0:T(1024)}, u32[]{:S(2)}) copy-start(f32[1024]{0:T(1024)} %get-tuple-element.475) | copy-start | bytes 12292
  185.2 12.4 %copy-start.4 = (f32[1024]{0:T(1024)S(1)}, f32[1024]{0:T(1024)}, u32[]{:S(2)}) copy-start(f32[1024]{0:T(1024)} %get-tuple-element.476) | copy-start | bytes 12292
  197.6 1.0 copy-start.7
  203.5 1.0 copy-start.7
  209.4 1.0 copy-start.7
  215.3 1.0 copy-start.7
  221.1 1.0 copy-start.7
  227.0 1.0 copy-start.7
  232.9 1.0 copy-start.7
  238.8 1.0 copy-start.7
Sparse Core Ops, SparseCore 0:
  10.7 44.1 all-gather.1
  85.4 96.8 all-reduce.1
where the time goes:
time: 290 us; the launch traced here: 289 us
  waiting for transfers between devices  141 us (49%)
  matrix products  74.8 us (26%)
  blocking collectives  30.9 us (11%)
  between operations  20.2 us (7%)
  other arithmetic  16.1 us (6%)
  local copies, waits for them, and re-layouts  4.69 us (2%)
    psum x1, waiting for transfers between devices, shards(): desk_pnl = lax.psum(partial_value, 'asset')  96.4 us
    all_gather x1, waiting for transfers between devices, shards(): shocks = lax.all_gather(local_shocks, 'asset', axis=0, tiled=True)  45 us
    psum x1, blocking collectives, shards(): lax.psum(jnp.sum(grad_load * grad_load) + jnp.sum(grad_conv * grad_conv),...  30.9 us
    dot_general x8, matrix products, pnl_one_block(): return jnp.dot(held, table, preferred_element_type=jnp.float32)  30.3 us
    dot_general x8, matrix products, exposure_of(): lax.dot_general(shock_rows, loadings, (((1,), (1,)), ((), ())), preferred...  22.1 us
    dot_general x8, matrix products, grad_one_block(): lax.dot_general(grad_exposure, shock_block, (((0,), (0,)), ((), ())), pre...  16.2 us
  transfers between devices with their start and end apart: 2, of which 2 were waited for; matrix products, arithmetic and copies ran while one was open for 0% of the time, Pallas kernels for 0%

commit v1 on v0

--- a/solution.py
+++ b/solution.py
@@ -141,7 +141,11 @@
     table = desk_table(desk_map)
     shocks = lax.all_gather(local_shocks, "asset", axis=0, tiled=True)
     partial_value = pnl_rows(shocks, loadings, convexity, holdings, table)
-    desk_pnl = lax.psum(partial_value, "asset")
+    desk_pnl = partial_value
+    for hop in (1, 2, 4, 8):
+        desk_pnl = desk_pnl + lax.ppermute(
+            desk_pnl, "asset", [(dev, dev ^ hop) for dev in range(16)]
+        )
     cotangent, allocation = tail_terms(desk_pnl, ranks, desk_prices)
     initial = (
         jnp.zeros((loadings.shape[0], loadings.shape[1]), jnp.float32),

time: 290 us -> 378 us (1.30)
  waiting for transfers between devices: 141 us -> 233 us
  matrix products: 74.8 us -> 69 us
  local copies, waits for them, and re-layouts: 4.69 us -> 0.89 us
    ppermute x0 -> x4, waiting for transfers between devices: none -> 188 us  [shards(): lax.ppermute(desk_pnl, 'asset', [(dev, dev ^ hop) for dev in range(16)])]
    psum x1 -> x0, waiting for transfers between devices: 96.4 us -> none  [shards(): desk_pnl = lax.psum(partial_value, 'asset')]
    dot_general x8, matrix products: 30.3 us -> 24.5 us  [pnl_one_block(): return jnp.dot(held, table, preferred_element_type=jnp.float32)]
    while x16 -> x0, local copies, waits for them, and re-layouts: 3.8 us -> none
  transfers between devices with their start and end apart: 2 -> 5, of which waited for: 2 -> 5; matrix products, arithmetic and copies ran while one was open for 0% -> 0% of each run, Pallas kernels for 0% -> 0%
where the time goes in v1:
time: 378 us; the launch traced here: 377 us
  waiting for transfers between devices  233 us (62%)
  matrix products  69 us (18%)
  blocking collectives  31.8 us (8%)
  between operations  20.2 us (5%)
  other arithmetic  19.1 us (5%)
    ppermute x4, waiting for transfers between devices, shards(): lax.ppermute(desk_pnl, 'asset', [(dev, dev ^ hop) for dev in range(16)])  188 us
    all_gather x1, waiting for transfers between devices, shards(): shocks = lax.all_gather(local_shocks, 'asset', axis=0, tiled=True)  45.1 us
    psum x1, blocking collectives, shards(): lax.psum(jnp.sum(grad_load * grad_load) + jnp.sum(grad_conv * grad_conv),...  31.8 us
    dot_general x8, matrix products, pnl_one_block(): return jnp.dot(held, table, preferred_element_type=jnp.float32)  24.5 us
    dot_general x8, matrix products, exposure_of(): lax.dot_general(shock_rows, loadings, (((1,), (1,)), ((), ())), preferred...  22.1 us
    dot_general x8, matrix products, grad_one_block(): lax.dot_general(grad_exposure, shock_block, (((0,), (0,)), ((), ())), pre...  16.2 us
  transfers between devices with their start and end apart: 5, of which 5 were waited for; matrix products, arithmetic and copies ran while one was open for 0% of the time, Pallas kernels for 0%

profile of v1, /device:TPU:0, one launch (start us, length us, event | category | flops | bytes accessed | tf_op | source)
XLA Modules:
  0.0 376.9 jit_solution(2119239122657014810)
XLA Ops:
  7.2 0.0 all-gather.2.cloned.1.call-start
  7.2 0.8 copy-done
  8.1 1.7 convolution_convert_fusion
  9.9 45.1 %all-gather.2.cloned.1.call-done = bf16[4096,256]{1,0:T(8,128)(2,1)} async-done(((bf16[256,256]{1,0:T(8,128)(2,1)}), bf16[4096,256]{1,0:T(8,128)(2,1)}) %all-gather.2.cloned.1.call-update) | async-done | bytes 2097168 | tf_op jit(solution)/shard_map/all_gather | solution.py:142
  54.9 24.7 %while.28 = (s32[]{:T(128)}, f32[8,512,128]{2,1,0:T(8,128)S(1)}, f32[1024]{0:T(1024)}, bf16[8,512,256]{2,1,0:T(8,128)(2,1)}, bf16[1024,256]{1,0:T(8,128)(2,1)}, /*index=5*/f32[1024]{0:T(1024)}, s32[1024]{0:T(1024)}, s32[]{:T(128)}) while((s32[]{:T(128)}, f32[8,512,128]{2,1,0:T(8,128)S(1)}, f32[1024]{0:T(1024)}, ...), condition=%wide.region_1.2_spmd.clone, body=%wide.region_0.1_spmd.clone.sunk | while | flops 410255360 | bytes 1061981 | solution.py:107
  54.9 3.1 fusion.70
  58.0 3.1 fusion.70
  61.1 3.1 fusion.70
  64.2 3.1 fusion.70
  67.3 3.1 fusion.70
  70.4 3.1 fusion.70
  73.5 3.1 fusion.70
  76.6 3.1 fusion.70
  79.7 0.3 collective-permute-start
  80.0 3.9 %collective-permute-done = f32[4096,128]{1,0:T(8,128)S(1)} collective-permute-done((f32[4096,128]{1,0:T(8,128)S(1)}, f32[4096,128]{1,0:T(8,128)S(1)}, u32[]{:S(2)}, u32[]{:S(2)}) %collective-permute-start) | collective-permute-done | bytes 2097184 | tf_op jit(solution)/shard_map/ppermute | solution.py:146
  83.9 0.3 bitcast_add_fusion
  84.2 0.6 collective-permute-start.1
  84.8 47.2 %collective-permute-done.1 = f32[4096,128]{1,0:T(8,128)S(1)} collective-permute-done((f32[4096,128]{1,0:T(8,128)S(1)}, f32[4096,128]{1,0:T(8,128)S(1)}, u32[]{:S(2)}, u32[]{:S(2)}) %collective-permute-start.1) | collective-permute-done | bytes 2097184 | tf_op jit(solution)/shard_map/ppermute | solution.py:146
  132.0 0.2 add.112
  132.2 0.4 collective-permute-start.2
  132.6 46.6 %collective-permute-done.2 = f32[4096,128]{1,0:T(8,128)S(1)} collective-permute-done((f32[4096,128]{1,0:T(8,128)S(1)}, f32[4096,128]{1,0:T(8,128)S(1)}, u32[]{:S(2)}, u32[]{:S(2)}) %collective-permute-start.2) | collective-permute-done | bytes 2097184 | tf_op jit(solution)/shard_map/ppermute | solution.py:146
  179.2 0.2 add.113
  179.4 0.9 collective-permute-start.3
  180.3 0.6 exponential_reduce_fusion
  181.0 90.3 %collective-permute-done.3 = f32[4096,128]{1,0:T(8,128)} collective-permute-done((f32[4096,128]{1,0:T(8,128)S(1)}, f32[4096,128]{1,0:T(8,128)}, u32[]{:S(2)}, u32[]{:S(2)}) %collective-permute-start.3) | collective-permute-done | bytes 2097184 | tf_op jit(solution)/shard_map/ppermute | solution.py:146
  271.2 4.0 %fusion.50 = (f32[]{:T(128)}, f32[4096]{0:T(1024)S(1)}, f32[4096,128]{1,0:T(8,128)}) fusion(f32[4096,128]{1,0:T(8,128)S(1)} %add.113, f32[4096,128]{1,0:T(8,128)} %collective-permute-done.3), kind=kLoop, calls=%fused_computation.74 | loop fusion | flops 1568767 | bytes 6307844 | tf_op jit(solution)/shard_map/reduce_sum | solution.py:50
  276.0 1.3 multiply_reduce_fusion.6
  277.9 0.7 fusion.52
  278.6 2.5 multiply_reduce_fusion
  281.1 0.6 multiply_reduce_fusion.4
  283.1 1.9 fusion.51
  286.3 0.7 divide_add_fusion
  287.0 1.9 multiply_convert_fusion.2
  288.9 43.1 %while.29 = (s32[]{:T(128)}, f32[1024,256]{1,0:T(8,128)S(1)}, f32[1024]{0:T(1024)S(1)}, f32[1024]{0:T(1024)S(1)}, bf16[8,512,128]{2,1,0:T(8,128)(2,1)S(1)}, /*in...) while((s32[]{:T(128)}, f32[1024,256]{1,0:T(8,128)S(1)}, ...), condition=%wide.region_15.16_spmd.clone, body=%wide.region_13.15_spmd.clone.sunk | while | flops 681313280 | bytes 13795468 | solution.py:129
  288.9 0.6 fusion.75
  289.5 2.8 fusion.76
  292.2 2.0 convolution_add_fusion.2
  294.3 0.5 fusion.75
  294.9 2.8 fusion.76
  297.6 2.0 convolution_add_fusion.2
  299.7 0.5 fusion.75
  300.3 2.8 fusion.76
  303.0 2.0 convolution_add_fusion.2
  305.1 0.5 fusion.75
  305.6 2.8 fusion.76
  308.4 2.0 convolution_add_fusion.2
  310.5 0.5 fusion.75
  311.0 2.8 fusion.76
  313.8 2.0 convolution_add_fusion.2
  315.9 0.5 fusion.75
  316.4 2.8 fusion.76
  319.2 2.0 convolution_add_fusion.2
  321.3 0.5 fusion.75
  321.8 2.8 fusion.76
  324.6 2.0 convolution_add_fusion.2
  326.6 0.5 fusion.75
  327.2 2.8 fusion.76
  330.0 2.0 convolution_add_fusion.2
  332.0 0.9 multiply_reduce_fusion.2
  332.9 0.6 multiply_reduce_fusion.7
  334.8 31.8 %psum.7 = f32[]{:T(128)} all-reduce(f32[]{:T(128)S(6)} %add.120), channel_id=1, replica_groups=mesh['groups'=2,'asset'=16] {'asset'}, use_global_device_ids=true, to_apply=%region_18.19 | all-reduce | flops 1 | bytes 8 | tf_op jit(solution)/shard_map/psum | solution.py:157
  367.3 0.6 broadcast_multiply_fusion.1
  367.9 1.0 broadcast_multiply_fusion
  369.0 1.1 negate_divide_fusion
  (27 shorter events, 0.1 us)
Async XLA Ops:
  7.2 0.9 copy-start
  7.2 47.8 %all-gather.2.cloned.1.call-start = ((), (), s32[]{:S(2)}) async-start(), calls=%async_computation | async-start | bytes 2228224 | tf_op jit(solution)/shard_map/all_gather | solution.py:142
  79.7 4.2 %collective-permute-start = (f32[4096,128]{1,0:T(8,128)S(1)}, f32[4096,128]{1,0:T(8,128)S(1)}, u32[]{:S(2)}, u32[]{:S(2)}) collective-permute-start(f32[4096,128]{1,0:T(8,128)S(1)} %bitcast.39), channel_id=1, source_target_pairs={{0,1},{1,0},{2,3},{3,2},{4,5},{5,4},{6,7},{7,6},{8,9},{9,8},{10,11... | collective-permute-start | bytes 6291464 | tf_op jit(solution)/shard_map/ppermute | solution.py:146
  84.2 47.8 %collective-permute-start.1 = (f32[4096,128]{1,0:T(8,128)S(1)}, f32[4096,128]{1,0:T(8,128)S(1)}, u32[]{:S(2)}, u32[]{:S(2)}) collective-permute-start(f32[4096,128]{1,0:T(8,128)S(1)} %bitcast_add_fusion), channel_id=1, source_target_pairs={{0,2},{1,3},{2,0},{3,1},{4,6},{5,7},{6,4},{7,5},{8,10},{9,11},{10,... | collective-permute-start | bytes 6291464 | tf_op jit(solution)/shard_map/ppermute | solution.py:146
  132.2 47.0 %collective-permute-start.2 = (f32[4096,128]{1,0:T(8,128)S(1)}, f32[4096,128]{1,0:T(8,128)S(1)}, u32[]{:S(2)}, u32[]{:S(2)}) collective-permute-start(f32[4096,128]{1,0:T(8,128)S(1)} %add.112), channel_id=1, source_target_pairs={{0,4},{1,5},{2,6},{3,7},{4,0},{5,1},{6,2},{7,3},{8,12},{9,13},{10,... | collective-permute-start | bytes 6291464 | tf_op jit(solution)/shard_map/ppermute | solution.py:146
  179.4 91.8 %collective-permute-start.3 = (f32[4096,128]{1,0:T(8,128)S(1)}, f32[4096,128]{1,0:T(8,128)}, u32[]{:S(2)}, u32[]{:S(2)}) collective-permute-start(f32[4096,128]{1,0:T(8,128)S(1)} %add.113), channel_id=1, source_target_pairs={{0,8},{1,9},{2,10},{3,11},{4,12},{5,13},{6,14},{7,15},{8,0},{9,1},... | collective-permute-start | bytes 6291464 | tf_op jit(solution)/shard_map/ppermute | solution.py:146
  180.9 95.0 %copy-start.4 = (s32[4096]{0:T(1024)S(1)}, s32[4096]{0:T(1024)}, u32[]{:S(2)}) copy-start(s32[4096]{0:T(1024)} %param.18) | copy-start | bytes 49156
  181.0 97.7 %copy-start.5 = (f32[128]{0:T(128)S(1)}, f32[128]{0:T(128)}, u32[]{:S(2)}) copy-start(f32[128]{0:T(128)} %param.19) | copy-start | bytes 1540
  275.2 13.6 %copy-start.1 = (s32[1024]{0:T(1024)S(1)}, s32[1024]{0:T(1024)}, u32[]{:S(2)}) copy-start(s32[1024]{0:T(1024)} %get-tuple-element.478) | copy-start | bytes 12292
  275.2 13.6 %copy-start.2 = (f32[1024]{0:T(1024)S(1)}, f32[1024]{0:T(1024)}, u32[]{:S(2)}) copy-start(f32[1024]{0:T(1024)} %get-tuple-element.479) | copy-start | bytes 12292
  275.2 13.6 %copy-start.3 = (f32[1024]{0:T(1024)S(1)}, f32[1024]{0:T(1024)}, u32[]{:S(2)}) copy-start(f32[1024]{0:T(1024)} %get-tuple-element.480) | copy-start | bytes 12292
  275.2 13.7 %copy-start.6 = (bf16[1024,256]{1,0:T(8,128)(2,1)S(1)}, bf16[1024,256]{1,0:T(8,128)(2,1)}, u32[]{:S(2)}) copy-start(bf16[1024,256]{1,0:T(8,128)(2,1)} %get-tuple-element.481) | copy-start | bytes 1572868
Sparse Core Ops, SparseCore 0:
  10.7 44.1 all-gather.1
